TPU v7x, 32 devices: a whole 2x2x4 slice. The times are simulated.
32 devices in a mesh: comp: 2 (over core), tile: 16 (over z, y, x).
Axes of the slice: x: 2, y: 2, z: 4, core: 2. Of those that a mesh axis runs over, the one named last changes fastest.
Arguments:
- state: float32 [2, 8, 256, 1024], P('comp', None, 'tile'), may hold values from -80 to 80, as said below
- basis: bfloat16 [12, 2, 8, 256, 1024], P(None, 'comp', None, 'tile'), may hold values from -4 to 4
- kappa: float32 [2, 256, 1024], P('comp', 'tile'), may hold values from 0.05 to 0.22
- vmix: float32 [2, 8, 8], P('comp'), may hold values from -1 to 1
- land_mask: int32 [256, 1024], P('tile'), may hold values 0 or 1
- send_rows: int32 [2, 16, 16, 8], P('comp', 'tile'), may hold values from 0 to 127
- recv_slots: int32 [2, 16, 128, 4], P('comp', 'tile'), may hold values from 0 to 127
- recv_weights: float32 [2, 16, 128, 4], P('comp', 'tile'), may hold values from 0.1 to 0.4
Outputs:
- direction: float32 [2, 8, 256, 1024], P('comp', None, 'tile')
- coefs: float32 [12], replicated
Inputs may be any that keep to these rules, and one draw needn't show every extreme that they name: `state`: the perturbation is noise plus a combination of the basis vectors.
All inputs are finite; a program needn't handle non-finite values. No bound on the sum of `land_mask` on one device may be relied on, other than what follows from the above.
Results may differ from a plain program's by a relative error of at most 0.0003.
Values sent between devices are 32-bit elements; how exact they have to be, the bound alone decides.
No kernel may reach another device: no remote copies, remote signals or barrier semaphores. Data moves between devices by JAX's collectives and lax.ppermute only.
A program may use at most 64 MiB of HBM per device.

v0:
```python
import jax
import jax.numpy as jnp
from jax import lax
from jax.sharding import PartitionSpec as P

FLUX = 4
VECS = 12


def extended(cells, sides, width):
    for axis, dim in sides:
        count = lax.axis_size(axis)
        ends = count - 1
        head = lax.slice_in_dim(cells, 0, width, axis=dim)
        tail = lax.slice_in_dim(cells, cells.shape[dim] - width, cells.shape[dim], axis=dim)
        cells = jnp.concatenate(
            [
                lax.ppermute(tail, axis, [(i, (i + 1) % count) for i in range(ends)]),
                cells,
                lax.ppermute(head, axis, [((i + 1) % count, i) for i in range(ends)]),
            ],
            axis=dim,
        )
    return cells


def from_partner(block, axis, stride):
    count = lax.axis_size(axis)
    route = []
    for low in range(count):
        high = low | 1 << stride
        if high != low and high < count:
            route += [(low, high), (high, low)]
    return lax.ppermute(block, axis, route)


def advance(x, kap, vert_mat, maskf, forced):
    padded = extended(x, (("tile", 1),), 1)
    lap = padded[:, 2:] + padded[:, :-2] + jnp.roll(x, 1, -1) + jnp.roll(x, -1, -1) - 4.0 * x
    vert = jnp.einsum("lm,mrq->lrq", vert_mat, x, precision=lax.Precision.HIGHEST)
    return maskf * (x + kap * lap + vert + forced)


def body(state, basis, kappa, vmix, land_mask, send_rows, recv_slots, recv_weights):
    comp_id = lax.axis_index("comp")
    x = state[0]
    levels, rows, cols = x.shape
    nblk = rows * cols // 128
    surface = x[:FLUX].reshape(FLUX, nblk, 128)
    bucket = surface[:, send_rows[0, 0]]
    moved = lax.all_to_all(bucket, "tile", split_axis=1, concat_axis=1, tiled=True)
    arrived = from_partner(moved, "comp", 0)
    flat = arrived.reshape(FLUX, -1, 128)
    picked = flat[:, recv_slots[0, 0]]
    imported = jnp.einsum(
        "ek,fekq->feq", recv_weights[0, 0], picked, precision=lax.Precision.HIGHEST
    )
    imported = imported.reshape(FLUX, rows, cols)
    forced = jnp.concatenate([imported, jnp.zeros((levels - FLUX, rows, cols), jnp.float32)], 0)
    maskf = jnp.where(comp_id == 0, land_mask.astype(jnp.float32), jnp.float32(1.0))
    for step in range(2):
        x = advance(x, kappa[0], vmix[0], maskf, forced)
    total = float(levels * rows * cols * lax.axis_size("comp") * lax.axis_size("tile"))
    vflat = x.reshape(-1)
    qmat = basis[:, 0].reshape(VECS, -1)
    local_dots = jnp.dot(
        qmat, vflat, precision=lax.Precision.HIGHEST, preferred_element_type=jnp.float32
    )
    local_gram = jnp.dot(qmat, qmat.T, preferred_element_type=jnp.float32)
    dots, squares, gram = lax.psum(
        (local_dots, jnp.sum(vflat * vflat), local_gram), ("comp", "tile")
    )
    coefs = dots / total
    remain = vflat - jnp.dot(
        coefs, qmat, precision=lax.Precision.HIGHEST, preferred_element_type=jnp.float32
    )
    normsq = (
        squares
        - 2.0 * total * jnp.sum(coefs * coefs)
        + jnp.dot(
            coefs,
            jnp.dot(gram, coefs, precision=lax.Precision.HIGHEST),
            precision=lax.Precision.HIGHEST,
        )
    )
    direction = remain / jnp.sqrt(normsq / total + 1e-06)
    return (direction.reshape(1, levels, rows, cols), coefs)


def solution(mesh):
    return jax.shard_map(
        body,
        mesh=mesh,
        in_specs=(
            P("comp", None, "tile", None),
            P(None, "comp", None, "tile", None),
            P("comp", "tile", None),
            P("comp", None, None),
            P("tile", None),
            P("comp", "tile", None, None),
            P("comp", "tile", None, None),
            P("comp", "tile", None, None),
        ),
        out_specs=(P("comp", None, "tile", None), P()),
        check_vma=False,
    )
```

profile of v0, /device:TPU:0, one launch (start us, length us, event | category | flops | bytes accessed | tf_op | source)
XLA Modules:
  0.0 113.7 jit_solution(10225340703240517486)
XLA Ops:
  0.7 1.4 %copy.38 = f32[1,8,16,1024]{3,1,2,0:T(8,128)S(1)} copy(f32[1,8,16,1024]{3,2,1,0:T(8,128)} %param.8) | data formatting | bytes 1048576 | tf_op args[0]
  2.0 1.3 %collective-permute-start = (f32[8,1,1024]{2,0,1:T(8,128)S(1)}, f32[8,1,1024]{2,0,1:T(8,128)S(1)}, u32[]{:S(2)}, u32[]{:S(2)}) collective-permute-start(f32[8,1,1024]{2,0,1:T(8,128)S(1)} %get-tuple-element.17), channel_id=1, source_target_pairs={{1,0},{2,1},{3,2},{4,3},{5,4},{6,5},{7,6},{8,7},{9,8},{10,9},{11,1... | collective-permute-start | bytes 98312 | tf_op jit(solution)/shard_map/ppermute | solution.py:20
  3.3 5.5 %collective-permute-start.1 = (f32[8,1,1024]{2,0,1:T(8,128)S(1)}, f32[8,1,1024]{2,0,1:T(8,128)S(1)}, u32[]{:S(2)}, u32[]{:S(2)}) collective-permute-start(f32[8,1,1024]{2,0,1:T(8,128)S(1)} %get-tuple-element.18), channel_id=1, source_target_pairs={{0,1},{1,2},{2,3},{3,4},{4,5},{5,6},{6,7},{7,8},{8,9},{9,10},{10,1... | collective-permute-start | bytes 98312 | tf_op jit(solution)/shard_map/ppermute | solution.py:18
  8.8 1.0 slice.68
  10.0 0.7 compare_select_fusion
  10.9 1.4 %gather_fusion = f32[128,4,128]{2,1,0:T(4,128)} fusion(f32[4,128,128]{2,0,1:T(4,128)S(1)} %copy.18, s32[1024]{0:T(1024)S(1)} %pad_clamp_fusion.1), kind=kCustom, calls=%fused_computation | custom fusion | bytes 524800 | tf_op jit(solution)/shard_map/gather | solution.py:50
  12.4 8.2 %all-to-all-start = ((f32[4,16,8,128]{3,0,2,1:T(4,128)}), f32[4,16,8,128]{3,0,2,1:T(4,128)S(1)}, u32[]{:S(2)}, u32[]{:S(2)}) async-start(f32[4,16,8,128]{3,0,2,1:T(4,128)} %bitcast.6), calls=%async_computation | async-start | bytes 524288 | tf_op jit(solution)/shard_map/all_to_all | solution.py:51
  20.6 0.7 compare_select_fusion.1
  21.7 2.3 %pad.27 = bf16[16,128,1024]{2,1,0:T(8,128)(2,1)S(1)} pad(bf16[12,128,1024]{2,1,0:T(8,128)(2,1)} %bitcast.89, bf16[]{:T(256)} %constant.53), padding=0_4x0_0x0_0 | pad | bytes 7340034
  24.0 4.3 %copy.30 = bf16[2,8,128,1024]{3,1,2,0:T(8,128)(2,1)} copy(bf16[2,8,128,1024]{3,2,1,0:T(8,128)(2,1)S(1)} %bitcast.81) | data formatting | bytes 8388608
  28.3 9.4 %fusion.7 = f32[12,12]{1,0:T(8,128)S(1)} fusion(bf16[12,8,16,1024]{3,2,1,0:T(8,128)(2,1)} %bitcast.90), kind=kOutput, calls=%fused_computation.11 | convolution fusion | flops 37748736 | bytes 3146304 | tf_op jit(solution)/shard_map/dot_general | solution.py:69
  38.0 1.3 %collective-permute-done.2 = f32[4,16,8,128]{3,0,2,1:T(4,128)S(1)} collective-permute-done((f32[4,16,8,128]{3,0,2,1:T(4,128)S(1)}, f32[4,16,8,128]{3,0,2,1:T(4,128)S(1)}, u32[]{:S(2)}, u32[]{:S(2)}) %collective-permute-start.2) | collective-permute-done | bytes 262176 | tf_op jit(solution)/shard_map/ppermute | solution.py:34
  39.3 2.3 %gather_fusion.1 = f32[512,4,128]{2,1,0:T(4,128)S(1)} fusion(f32[4,128,128]{2,0,1:T(4,128)S(1)} %bitcast.88, s32[1024]{0:T(1024)S(1)} %pad_clamp_fusion), kind=kCustom, calls=%fused_computation.1 | custom fusion | bytes 2099200 | tf_op jit(solution)/shard_map/gather | solution.py:54
  41.6 2.0 %fusion.11 = f32[128,1,4,128]{3,1,2,0:T(1,128)S(1)} fusion(f32[128,4,1,1]{1,2,3,0:T(1,128)S(1)} %copy.24, f32[4,128,4,128]{3,0,2,1:T(4,128)S(1)} %bitcast.87), kind=kOutput, calls=%fused_computation.15 | convolution fusion | flops 3145728 | bytes 1312768 | tf_op jit(solution)/shard_map/ek,fekq->feq/dot_general | solution.py:55
  43.7 0.9 fusion.6
  44.8 1.3 %collective-permute-start.3 = (f32[8,1,1024]{2,0,1:T(8,128)S(1)}, f32[8,1,1024]{2,0,1:T(8,128)S(1)}, u32[]{:S(2)}, u32[]{:S(2)}) collective-permute-start(f32[8,1,1024]{2,0,1:T(8,128)S(1)} %get-tuple-element.11), channel_id=1, source_target_pairs={{1,0},{2,1},{3,2},{4,3},{5,4},{6,5},{7,6},{8,7},{9,8},{10,9},{11,1... | collective-permute-start | bytes 98312 | tf_op jit(solution)/shard_map/ppermute | solution.py:20
  46.1 4.5 %collective-permute-start.4 = (f32[8,1,1024]{2,0,1:T(8,128)S(1)}, f32[8,1,1024]{2,0,1:T(8,128)S(1)}, u32[]{:S(2)}, u32[]{:S(2)}) collective-permute-start(f32[8,1,1024]{2,0,1:T(8,128)S(1)} %get-tuple-element.12), channel_id=1, source_target_pairs={{0,1},{1,2},{2,3},{3,4},{4,5},{5,6},{6,7},{7,8},{8,9},{9,10},{10,1... | collective-permute-start | bytes 98312 | tf_op jit(solution)/shard_map/ppermute | solution.py:18
  50.7 1.5 %collective-permute-done.4 = f32[8,1,1024]{2,0,1:T(8,128)S(1)} collective-permute-done((f32[8,1,1024]{2,0,1:T(8,128)S(1)}, f32[8,1,1024]{2,0,1:T(8,128)S(1)}, u32[]{:S(2)}, u32[]{:S(2)}) %collective-permute-start.4) | collective-permute-done | bytes 32800 | tf_op jit(solution)/shard_map/ppermute | solution.py:18
  52.2 1.4 %multiply_reduce_fusion = (f32[]{:T(128)}, f32[8,16,1024]{2,0,1:T(8,128)S(1)}) fusion(f32[4,16,1024]{2,0,1:T(4,128)S(1)} %bitcast.94, f32[8,16,1024]{2,0,1:T(8,128)S(1)} %fusion.6, f32[1,8,8]{2,1,0:T(8,128)S(1)} %copy-done, f32[8,16,1]{2,0,1:T(8,128)S(1)} %get-tuple-element.9, f32[8,16,1023]{2,0,1:T(8,128)S(1)} %get-tuple-element.7, ...), kind=kOutput, calls=%fused_computation.35 | convolution fusion | flops 14680063 | bytes 2556164 | tf_op jit(solution)/shard_map/lm,mrq->lrq/dot_general | solution.py:40
  54.6 6.5 %convolution_bitcast_fusion.1 = f32[12]{0:T(128)S(1)} fusion(f32[131072,1]{0,1:T(1,128)S(1)} %reshape.109, bf16[12,131072]{1,0:T(8,128)(2,1)} %bitcast.79), kind=kOutput, calls=%fused_computation.12 | convolution fusion | flops 18874368 | bytes 3670064 | tf_op jit(solution)/shard_map/dot_general | solution.py:66
  61.1 44.3 %all-reduce.1 = (f32[12]{0:T(128)S(1)}, f32[]{:T(128)}, f32[12,12]{1,0:T(8,128)S(1)}) all-reduce(f32[12]{0:T(128)S(1)} %convolution_bitcast_fusion.1, f32[]{:T(128)} %get-tuple-element.19, f32[12,12]{1,0:T(8,128)S(1)} %fusion.7), channel_id=1, replica_groups=mesh['comp'=2,'tile'=16] {'comp','tile'}, use_global_device_ids=true, to_apply=%region_0.1 | all-reduce | flops 157 | bytes 1256 | tf_op jit(solution)/shard_map/psum | solution.py:70
  106.0 4.0 %fusion.29 = f32[1,131072]{1,0:T(1,128)S(1)} fusion(bf16[12,131072]{1,0:T(8,128)(2,1)} %bitcast.80, f32[12]{0:T(128)S(1)} %get-tuple-element.6), kind=kOutput, calls=%fused_computation.45 | convolution fusion | flops 18874368 | bytes 3670064 | tf_op jit(solution)/shard_map/dot_general | solution.py:74
  110.0 0.8 fusion.13
  112.8 0.9 reshape.87
  (36 shorter events, 3.1 us)
Async XLA Ops:
  0.6 43.0 %copy-start = (f32[1,8,8]{2,1,0:T(8,128)S(1)}, f32[1,8,8]{2,1,0:T(8,128)}, u32[]{:S(2)}) copy-start(f32[1,8,8]{2,1,0:T(8,128)} %param.11) | copy-start | bytes 772
  0.6 20.9 %copy-start.3 = (f32[1,1,128,4]{2,3,1,0:T(4,128)S(1)}, f32[1,1,128,4]{2,3,1,0:T(4,128)}, u32[]{:S(2)}) copy-start(f32[1,1,128,4]{2,3,1,0:T(4,128)} %param.15) | copy-start | bytes 6148
  2.0 41.6 %collective-permute-start = (f32[8,1,1024]{2,0,1:T(8,128)S(1)}, f32[8,1,1024]{2,0,1:T(8,128)S(1)}, u32[]{:S(2)}, u32[]{:S(2)}) collective-permute-start(f32[8,1,1024]{2,0,1:T(8,128)S(1)} %get-tuple-element.17), channel_id=1, source_target_pairs={{1,0},{2,1},{3,2},{4,3},{5,4},{6,5},{7,6},{8,7},{9,8},{10,9},{11,1... | collective-permute-start | bytes 98312 | tf_op jit(solution)/shard_map/ppermute | solution.py:20
  3.3 40.3 %collective-permute-start.1 = (f32[8,1,1024]{2,0,1:T(8,128)S(1)}, f32[8,1,1024]{2,0,1:T(8,128)S(1)}, u32[]{:S(2)}, u32[]{:S(2)}) collective-permute-start(f32[8,1,1024]{2,0,1:T(8,128)S(1)} %get-tuple-element.18), channel_id=1, source_target_pairs={{0,1},{1,2},{2,3},{3,4},{4,5},{5,6},{6,7},{7,8},{8,9},{9,10},{10,1... | collective-permute-start | bytes 98312 | tf_op jit(solution)/shard_map/ppermute | solution.py:18
  12.4 25.4 %all-to-all-start = ((f32[4,16,8,128]{3,0,2,1:T(4,128)}), f32[4,16,8,128]{3,0,2,1:T(4,128)S(1)}, u32[]{:S(2)}, u32[]{:S(2)}) async-start(f32[4,16,8,128]{3,0,2,1:T(4,128)} %bitcast.6), calls=%async_computation | async-start | bytes 524288 | tf_op jit(solution)/shard_map/all_to_all | solution.py:51
  24.0 4.3 %copy-start.1 = (s32[16,1024]{1,0:T(8,128)S(1)}, s32[16,1024]{1,0:T(8,128)}, u32[]{:S(2)}) copy-start(s32[16,1024]{1,0:T(8,128)} %param.12) | copy-start | bytes 196612
  37.7 5.9 %copy-start.4 = (f32[1,16,1024]{2,1,0:T(8,128)S(1)}, f32[1,16,1024]{2,1,0:T(8,128)}, u32[]{:S(2)}) copy-start(f32[1,16,1024]{2,1,0:T(8,128)} %param.10) | copy-start | bytes 196612
  37.7 1.6 %collective-permute-start.2 = (f32[4,16,8,128]{3,0,2,1:T(4,128)S(1)}, f32[4,16,8,128]{3,0,2,1:T(4,128)S(1)}, u32[]{:S(2)}, u32[]{:S(2)}) collective-permute-start(f32[4,16,8,128]{3,0,2,1:T(4,128)S(1)} %all-to-all-done), channel_id=1, source_target_pairs={{0,16},{16,0},{1,17},{17,1},{2,18},{18,2},{3,19},{19,3},{4,20},{20... | collective-permute-start | bytes 786440 | tf_op jit(solution)/shard_map/ppermute | solution.py:34
  44.8 5.9 %collective-permute-start.3 = (f32[8,1,1024]{2,0,1:T(8,128)S(1)}, f32[8,1,1024]{2,0,1:T(8,128)S(1)}, u32[]{:S(2)}, u32[]{:S(2)}) collective-permute-start(f32[8,1,1024]{2,0,1:T(8,128)S(1)} %get-tuple-element.11), channel_id=1, source_target_pairs={{1,0},{2,1},{3,2},{4,3},{5,4},{6,5},{7,6},{8,7},{9,8},{10,9},{11,1... | collective-permute-start | bytes 98312 | tf_op jit(solution)/shard_map/ppermute | solution.py:20
  46.1 6.1 %collective-permute-start.4 = (f32[8,1,1024]{2,0,1:T(8,128)S(1)}, f32[8,1,1024]{2,0,1:T(8,128)S(1)}, u32[]{:S(2)}, u32[]{:S(2)}) collective-permute-start(f32[8,1,1024]{2,0,1:T(8,128)S(1)} %get-tuple-element.12), channel_id=1, source_target_pairs={{0,1},{1,2},{2,3},{3,4},{4,5},{5,6},{6,7},{7,8},{8,9},{9,10},{10,1... | collective-permute-start | bytes 98312 | tf_op jit(solution)/shard_map/ppermute | solution.py:18
  106.0 6.8 %copy-start.2 = (f32[12]{0:T(128)}, f32[12]{0:T(128)S(1)}, u32[]{:S(2)}) copy-start(f32[12]{0:T(128)S(1)} %get-tuple-element.6) | copy-start | bytes 148
where the time goes:
time: 114 us
  blocking collectives  44.3 us (39%)
  matrix products  25 us (22%)
  starting transfers between devices  20.9 us (18%)
  local copies, waits for them, and re-layouts  15.8 us (14%)
  waiting for transfers between devices  2.82 us (2%)
  between operations  2.77 us (2%)
  other arithmetic  2.05 us (2%)
    psum x1, blocking collectives, body(): lax.psum((local_dots, jnp.sum(vflat * vflat), local_gram), ('comp', 'tile'))  44.3 us
    ppermute x2, starting transfers between devices, extended(): lax.ppermute(tail, axis, [(i, (i + 1) % count) for i in range(ends)])  10 us
    dot_general x1, matrix products, body(): local_gram = jnp.dot(qmat, qmat.T, preferred_element_type=jnp.float32)  9.43 us
    all_to_all x1, starting transfers between devices, body(): lax.all_to_all(bucket, 'tile', split_axis=1, concat_axis=1, tiled=True)  8.18 us
    unnamed x14, local copies, waits for them, and re-layouts  8.08 us
    dot_general x1, matrix products, body(): jnp.dot(qmat, vflat, precision=lax.Precision.HIGHEST, preferred_element_t...  6.49 us
    dot_general x1, matrix products, body(): jnp.dot(coefs, qmat, precision=lax.Precision.HIGHEST, preferred_element_t...  4 us
    ppermute x2, starting transfers between devices, extended(): lax.ppermute(head, axis, [((i + 1) % count, i) for i in range(ends)])  2.58 us
  transfers between devices with their start and end apart: 6, of which 2 were waited for; matrix products, arithmetic and copies ran while one was open for 22% of the time, Pallas kernels for 0%

commit v1 on v0

--- a/solution.py
+++ b/solution.py
@@ -48,7 +48,10 @@
     nblk = rows * cols // 128
     surface = x[:FLUX].reshape(FLUX, nblk, 128)
     bucket = surface[:, send_rows[0, 0]]
-    moved = lax.all_to_all(bucket, "tile", split_axis=1, concat_axis=1, tiled=True)
+    moved = jnp.concatenate(
+        lax.all_to_all(jnp.stack(jnp.split(bucket, lax.axis_size("tile"), axis=1)), "tile", 0, 0),
+        axis=1,
+    )
     arrived = from_partner(moved, "comp", 0)
     flat = arrived.reshape(FLUX, -1, 128)
     picked = flat[:, recv_slots[0, 0]]

time: 114 us -> 124 us (1.088)
  local copies, waits for them, and re-layouts: 15.8 us -> 25.1 us
    unnamed x14 -> x31, local copies, waits for them, and re-layouts: 8.08 us -> 17.2 us
  transfers between devices with their start and end apart: 6 -> 6, of which waited for: 2 -> 2; matrix products, arithmetic and copies ran while one was open for 22% -> 18% of each run, Pallas kernels for 0% -> 0%
where the time goes in v1:
time: 124 us; the launch traced here: 123 us
  blocking collectives  45.1 us (36%)
  local copies, waits for them, and re-layouts  25.1 us (20%)
  matrix products  25 us (20%)
  starting transfers between devices  20.9 us (17%)
  waiting for transfers between devices  2.97 us (2%)
  between operations  2.94 us (2%)
  other arithmetic  1.44 us (1%)
    psum x1, blocking collectives, body(): lax.psum((local_dots, jnp.sum(vflat * vflat), local_gram), ('comp', 'tile'))  45.1 us
    unnamed x31, local copies, waits for them, and re-layouts  17.2 us
    ppermute x2, starting transfers between devices, extended(): lax.ppermute(tail, axis, [(i, (i + 1) % count) for i in range(ends)])  9.91 us
    dot_general x1, matrix products, body(): local_gram = jnp.dot(qmat, qmat.T, preferred_element_type=jnp.float32)  9.43 us
    all_to_all x1, starting transfers between devices, body(): lax.all_to_all(jnp.stack(jnp.split(bucket, lax.axis_size('tile'), axis=1)...  8.34 us
    dot_general x1, matrix products, body(): jnp.dot(qmat, vflat, precision=lax.Precision.HIGHEST, preferred_element_t...  6.49 us
    dot_general x1, matrix products, body(): jnp.dot(coefs, qmat, precision=lax.Precision.HIGHEST, preferred_element_t...  4 us
    ppermute x2, starting transfers between devices, extended(): lax.ppermute(head, axis, [((i + 1) % count, i) for i in range(ends)])  2.58 us
  transfers between devices with their start and end apart: 6, of which 2 were waited for; matrix products, arithmetic and copies ran while one was open for 18% of the time, Pallas kernels for 0%

profile of v1, /device:TPU:0, one launch (start us, length us, event | category | flops | bytes accessed | tf_op | source)
XLA Modules:
  0.0 123.5 jit_solution(14271564420473378243)
XLA Ops:
  0.7 1.0 slice.68
  1.9 0.7 compare_select_fusion
  2.8 0.8 gather_fusion
  13.3 8.3 %all-to-all-start = ((f32[16,4,1,8,128]{4,3,1,2,0:T(8,128)}), f32[16,4,1,8,128]{4,3,1,2,0:T(8,128)S(1)}, u32[]{:S(2)}, u32[]{:S(2)}) async-start(f32[16,4,1,8,128]{4,3,1,2,0:T(8,128)} %constant_dynamic-update-slice_fusion), calls=%async_computation | async-start | bytes 524288 | tf_op jit(solution)/shard_map/all_to_all | solution.py:52
  21.6 1.4 %copy.99 = f32[1,8,16,1024]{3,1,2,0:T(8,128)S(1)} copy(f32[1,8,16,1024]{3,2,1,0:T(8,128)} %param.8) | data formatting | bytes 1048576 | tf_op args[0]
  23.0 1.3 %collective-permute-start = (f32[8,1,1024]{2,0,1:T(8,128)S(1)}, f32[8,1,1024]{2,0,1:T(8,128)S(1)}, u32[]{:S(2)}, u32[]{:S(2)}) collective-permute-start(f32[8,1,1024]{2,0,1:T(8,128)S(1)} %get-tuple-element.17), channel_id=1, source_target_pairs={{1,0},{2,1},{3,2},{4,3},{5,4},{6,5},{7,6},{8,7},{9,8},{10,9},{11,1... | collective-permute-start | bytes 98312 | tf_op jit(solution)/shard_map/ppermute | solution.py:20
  24.3 4.5 %collective-permute-start.1 = (f32[8,1,1024]{2,0,1:T(8,128)S(1)}, f32[8,1,1024]{2,0,1:T(8,128)S(1)}, u32[]{:S(2)}, u32[]{:S(2)}) collective-permute-start(f32[8,1,1024]{2,0,1:T(8,128)S(1)} %get-tuple-element.18), channel_id=1, source_target_pairs={{0,1},{1,2},{2,3},{3,4},{4,5},{5,6},{6,7},{7,8},{8,9},{9,10},{10,1... | collective-permute-start | bytes 98312 | tf_op jit(solution)/shard_map/ppermute | solution.py:18
  29.3 2.3 %pad.27 = bf16[16,128,1024]{2,1,0:T(8,128)(2,1)S(1)} pad(bf16[12,128,1024]{2,1,0:T(8,128)(2,1)} %bitcast.158, bf16[]{:T(256)} %constant.69), padding=0_4x0_0x0_0 | pad | bytes 7340034
  31.6 4.3 %copy.89 = bf16[2,8,128,1024]{3,1,2,0:T(8,128)(2,1)} copy(bf16[2,8,128,1024]{3,2,1,0:T(8,128)(2,1)S(1)} %bitcast.151) | data formatting | bytes 8388608
  35.9 9.4 %fusion.7 = f32[12,12]{1,0:T(8,128)S(1)} fusion(bf16[12,8,16,1024]{3,2,1,0:T(8,128)(2,1)} %bitcast.159), kind=kOutput, calls=%fused_computation.11 | convolution fusion | flops 37748736 | bytes 3146304 | tf_op jit(solution)/shard_map/dot_general | solution.py:72
  45.7 1.3 %collective-permute-done.2 = f32[4,16,8,128]{3,2,1,0:T(8,128)S(1)} collective-permute-done((f32[4,16,8,128]{3,2,1,0:T(8,128)S(1)}, f32[4,16,8,128]{3,2,1,0:T(8,128)S(1)}, u32[]{:S(2)}, u32[]{:S(2)}) %collective-permute-start.2) | collective-permute-done | bytes 262176 | tf_op jit(solution)/shard_map/ppermute | solution.py:34
  47.2 2.3 %gather_fusion.1 = f32[512,4,128]{2,1,0:T(4,128)S(1)} fusion(f32[4,128,128]{2,0,1:T(4,128)S(1)} %copy.78, s32[1024]{0:T(1024)S(1)} %pad_clamp_fusion), kind=kCustom, calls=%fused_computation.1 | custom fusion | bytes 2099200 | tf_op jit(solution)/shard_map/gather | solution.py:57
  49.4 2.0 %fusion.11 = f32[128,1,4,128]{3,1,2,0:T(1,128)S(1)} fusion(f32[128,4,1,1]{1,2,3,0:T(1,128)S(1)} %copy.83, f32[4,128,4,128]{3,0,2,1:T(4,128)S(1)} %bitcast.157), kind=kOutput, calls=%fused_computation.15 | convolution fusion | flops 3145728 | bytes 1312768 | tf_op jit(solution)/shard_map/ek,fekq->feq/dot_general | solution.py:58
  51.5 0.9 fusion.6
  52.6 1.3 %collective-permute-start.3 = (f32[8,1,1024]{2,0,1:T(8,128)S(1)}, f32[8,1,1024]{2,0,1:T(8,128)S(1)}, u32[]{:S(2)}, u32[]{:S(2)}) collective-permute-start(f32[8,1,1024]{2,0,1:T(8,128)S(1)} %get-tuple-element.11), channel_id=1, source_target_pairs={{1,0},{2,1},{3,2},{4,3},{5,4},{6,5},{7,6},{8,7},{9,8},{10,9},{11,1... | collective-permute-start | bytes 98312 | tf_op jit(solution)/shard_map/ppermute | solution.py:20
  53.9 5.4 %collective-permute-start.4 = (f32[8,1,1024]{2,0,1:T(8,128)S(1)}, f32[8,1,1024]{2,0,1:T(8,128)S(1)}, u32[]{:S(2)}, u32[]{:S(2)}) collective-permute-start(f32[8,1,1024]{2,0,1:T(8,128)S(1)} %get-tuple-element.12), channel_id=1, source_target_pairs={{0,1},{1,2},{2,3},{3,4},{4,5},{5,6},{6,7},{7,8},{8,9},{9,10},{10,1... | collective-permute-start | bytes 98312 | tf_op jit(solution)/shard_map/ppermute | solution.py:18
  59.3 1.6 %collective-permute-done.4 = f32[8,1,1024]{2,0,1:T(8,128)S(1)} collective-permute-done((f32[8,1,1024]{2,0,1:T(8,128)S(1)}, f32[8,1,1024]{2,0,1:T(8,128)S(1)}, u32[]{:S(2)}, u32[]{:S(2)}) %collective-permute-start.4) | collective-permute-done | bytes 32800 | tf_op jit(solution)/shard_map/ppermute | solution.py:18
  61.0 1.4 %multiply_reduce_fusion = (f32[]{:T(128)}, f32[8,16,1024]{2,0,1:T(8,128)S(1)}) fusion(f32[4,16,1024]{2,0,1:T(4,128)S(1)} %bitcast.182, f32[8,16,1024]{2,0,1:T(8,128)S(1)} %fusion.6, f32[1,8,8]{2,1,0:T(8,128)S(1)} %copy-done, f32[8,16,1]{2,0,1:T(8,128)S(1)} %get-tuple-element.9, f32[8,16,1023]{2,0,1:T(8,128)S(1)} %get-tuple-element.7, ...), kind=kOutput, calls=%fused_computation.35 | convolution fusion | flops 14680063 | bytes 2556164 | tf_op jit(solution)/shard_map/lm,mrq->lrq/dot_general | solution.py:40
  63.4 6.5 %convolution_bitcast_fusion.1 = f32[12]{0:T(128)S(1)} fusion(f32[131072,1]{0,1:T(1,128)S(1)} %reshape.117, bf16[12,131072]{1,0:T(8,128)(2,1)} %bitcast.149), kind=kOutput, calls=%fused_computation.12 | convolution fusion | flops 18874368 | bytes 3670064 | tf_op jit(solution)/shard_map/dot_general | solution.py:69
  69.9 45.1 %all-reduce.1 = (f32[12]{0:T(128)S(1)}, f32[]{:T(128)}, f32[12,12]{1,0:T(8,128)S(1)}) all-reduce(f32[12]{0:T(128)S(1)} %convolution_bitcast_fusion.1, f32[]{:T(128)} %get-tuple-element.19, f32[12,12]{1,0:T(8,128)S(1)} %fusion.7), channel_id=1, replica_groups=mesh['comp'=2,'tile'=16] {'comp','tile'}, use_global_device_ids=true, to_apply=%region_0.1 | all-reduce | flops 157 | bytes 1256 | tf_op jit(solution)/shard_map/psum | solution.py:73
  115.0 0.7 multiply_reduce_fusion.1
  115.7 4.0 %fusion.29 = f32[1,131072]{1,0:T(1,128)S(1)} fusion(bf16[12,131072]{1,0:T(8,128)(2,1)} %bitcast.150, f32[12]{0:T(128)S(1)} %get-tuple-element.6), kind=kOutput, calls=%fused_computation.79 | convolution fusion | flops 18874368 | bytes 3670064 | tf_op jit(solution)/shard_map/dot_general | solution.py:77
  119.7 0.8 fusion.13
  122.6 0.9 reshape.95
  (57 shorter events, 12.4 us)
Async XLA Ops:
  0.6 50.8 %copy-start = (f32[1,8,8]{2,1,0:T(8,128)S(1)}, f32[1,8,8]{2,1,0:T(8,128)}, u32[]{:S(2)}) copy-start(f32[1,8,8]{2,1,0:T(8,128)} %param.11) | copy-start | bytes 772
  0.6 28.3 %copy-start.4 = (s32[1,1,128,4]{2,3,1,0:T(4,128)S(1)}, s32[1,1,128,4]{2,3,1,0:T(4,128)}, u32[]{:S(2)}) copy-start(s32[1,1,128,4]{2,3,1,0:T(4,128)} %param.14) | copy-start | bytes 6148
  0.7 28.5 %copy-start.3 = (f32[1,1,128,4]{2,3,1,0:T(4,128)S(1)}, f32[1,1,128,4]{2,3,1,0:T(4,128)}, u32[]{:S(2)}) copy-start(f32[1,1,128,4]{2,3,1,0:T(4,128)} %param.15) | copy-start | bytes 6148
  13.3 32.1 %all-to-all-start = ((f32[16,4,1,8,128]{4,3,1,2,0:T(8,128)}), f32[16,4,1,8,128]{4,3,1,2,0:T(8,128)S(1)}, u32[]{:S(2)}, u32[]{:S(2)}) async-start(f32[16,4,1,8,128]{4,3,1,2,0:T(8,128)} %constant_dynamic-update-slice_fusion), calls=%async_computation | async-start | bytes 524288 | tf_op jit(solution)/shard_map/all_to_all | solution.py:52
  23.0 28.5 %collective-permute-start = (f32[8,1,1024]{2,0,1:T(8,128)S(1)}, f32[8,1,1024]{2,0,1:T(8,128)S(1)}, u32[]{:S(2)}, u32[]{:S(2)}) collective-permute-start(f32[8,1,1024]{2,0,1:T(8,128)S(1)} %get-tuple-element.17), channel_id=1, source_target_pairs={{1,0},{2,1},{3,2},{4,3},{5,4},{6,5},{7,6},{8,7},{9,8},{10,9},{11,1... | collective-permute-start | bytes 98312 | tf_op jit(solution)/shard_map/ppermute | solution.py:20
  24.3 27.2 %collective-permute-start.1 = (f32[8,1,1024]{2,0,1:T(8,128)S(1)}, f32[8,1,1024]{2,0,1:T(8,128)S(1)}, u32[]{:S(2)}, u32[]{:S(2)}) collective-permute-start(f32[8,1,1024]{2,0,1:T(8,128)S(1)} %get-tuple-element.18), channel_id=1, source_target_pairs={{0,1},{1,2},{2,3},{3,4},{4,5},{5,6},{6,7},{7,8},{8,9},{9,10},{10,1... | collective-permute-start | bytes 98312 | tf_op jit(solution)/shard_map/ppermute | solution.py:18
  31.6 4.3 %copy-start.1 = (s32[16,1024]{1,0:T(8,128)S(1)}, s32[16,1024]{1,0:T(8,128)}, u32[]{:S(2)}) copy-start(s32[16,1024]{1,0:T(8,128)} %param.12) | copy-start | bytes 196612
  45.3 6.1 %copy-start.5 = (f32[1,16,1024]{2,1,0:T(8,128)S(1)}, f32[1,16,1024]{2,1,0:T(8,128)}, u32[]{:S(2)}) copy-start(f32[1,16,1024]{2,1,0:T(8,128)} %param.10) | copy-start | bytes 196612
  45.4 1.6 %collective-permute-start.2 = (f32[4,16,8,128]{3,2,1,0:T(8,128)S(1)}, f32[4,16,8,128]{3,2,1,0:T(8,128)S(1)}, u32[]{:S(2)}, u32[]{:S(2)}) collective-permute-start(f32[4,16,8,128]{3,2,1,0:T(8,128)S(1)} %bitcast.179), channel_id=1, source_target_pairs={{0,16},{16,0},{1,17},{17,1},{2,18},{18,2},{3,19},{19,3},{4,20},{20... | collective-permute-start | bytes 786440 | tf_op jit(solution)/shard_map/ppermute | solution.py:34
  52.6 6.8 %collective-permute-start.3 = (f32[8,1,1024]{2,0,1:T(8,128)S(1)}, f32[8,1,1024]{2,0,1:T(8,128)S(1)}, u32[]{:S(2)}, u32[]{:S(2)}) collective-permute-start(f32[8,1,1024]{2,0,1:T(8,128)S(1)} %get-tuple-element.11), channel_id=1, source_target_pairs={{1,0},{2,1},{3,2},{4,3},{5,4},{6,5},{7,6},{8,7},{9,8},{10,9},{11,1... | collective-permute-start | bytes 98312 | tf_op jit(solution)/shard_map/ppermute | solution.py:20
  53.9 7.1 %collective-permute-start.4 = (f32[8,1,1024]{2,0,1:T(8,128)S(1)}, f32[8,1,1024]{2,0,1:T(8,128)S(1)}, u32[]{:S(2)}, u32[]{:S(2)}) collective-permute-start(f32[8,1,1024]{2,0,1:T(8,128)S(1)} %get-tuple-element.12), channel_id=1, source_target_pairs={{0,1},{1,2},{2,3},{3,4},{4,5},{5,6},{6,7},{7,8},{8,9},{9,10},{10,1... | collective-permute-start | bytes 98312 | tf_op jit(solution)/shard_map/ppermute | solution.py:18
  115.7 6.9 %copy-start.2 = (f32[12]{0:T(128)}, f32[12]{0:T(128)S(1)}, u32[]{:S(2)}) copy-start(f32[12]{0:T(128)S(1)} %get-tuple-element.6) | copy-start | bytes 148
